TPU v7x, 512 devices: a whole 4x8x8 slice. The times are simulated.
512 devices in a mesh: tok: 128 (over z, y, core), head: 4 (over x).
Axes of the slice: x: 4, y: 8, z: 8, core: 2. Of those that a mesh axis runs over, the one named last changes fastest.
Arguments:
- tokens: bfloat16 [16384, 1536], P('tok'), may hold values from -6 to 6
- norm_gain: bfloat16 [1536], replicated, may hold values from 0.099609375 to 1.8984375
- w_query: bfloat16 [1536, 1536], P('tok', 'head')
- w_keyval: bfloat16 [1536, 256], P('tok')
- w_out: bfloat16 [1536, 1536], P('head', 'tok'), may hold values from -0.5 to 0.5
- segment_ids: int32 [16384], P('tok'), may hold values from 0 to 30, as said below
- lengths: int32 [31], replicated, may hold values from 128 to 1024, as said below
- member_prompt: int32 [384], P('head'), may hold values from 0 to 30
Outputs:
- mixed: bfloat16 [16384, 1536], P('tok', 'head')
- cycle_cache: bfloat16 [384, 1024, 256], P('head', 'tok')
Inputs may be any that keep to these rules, and one draw needn't show every extreme that they name: The prompts lie end to end in the order of lengths and their lengths sum to 16384; one prompt has exactly 1024 tokens and one exactly 128. `segment_ids`: segment_ids_t is the prompt that holds token t under lengths, so it never falls.
All inputs are finite; a program needn't handle non-finite values.
Results may differ from a plain program's by a relative error of at most 0.013.
Values may be sent and summed in bfloat16 or wider, within the bound.
No kernel may reach another device: no remote copies, remote signals or barrier semaphores. Data moves between devices by JAX's collectives and lax.ppermute only.
A program may use at most 64 MiB of HBM per device.

v0:
```python
import math
import jax
import jax.numpy as jnp
from jax import lax
from jax.sharding import PartitionSpec as P

HD = 128
WINDOW = 1024


def shifted(block, axis, distance):
    devices = range(lax.axis_size(axis))
    route = [(i - distance, i) for i in devices if i - distance in devices]
    return lax.ppermute(block, axis, route)


def rotate(values, positions):
    half_width = values.shape[-1] // 2
    frequency = 10000.0 ** (-(jnp.arange(half_width, dtype=jnp.float32) * 2.0 / values.shape[-1]))
    angles = positions.astype(jnp.float32)[:, None] * frequency[None, :]
    cosine = jnp.cos(angles)[:, None, :]
    sine_values = jnp.sin(angles)[:, None, :]
    front_half = values[..., :half_width]
    back_half = values[..., half_width:]
    return jnp.concatenate(
        [
            front_half * cosine - back_half * sine_values,
            back_half * cosine + front_half * sine_values,
        ],
        axis=-1,
    )


def lookup_table(segments, table):
    matches = segments[:, None] == jnp.arange(table.shape[0], dtype=jnp.int32)[None, :]
    return jnp.sum(jnp.where(matches, table[None, :], 0), axis=1)


def per_device(tokens, norm_gain, w_query, w_keyval, w_out, segment_ids, lengths, member_prompt):
    shard_rows = tokens.shape[0]
    heads_here = w_query.shape[1] // HD
    devices = lax.axis_size("tok")
    tok_index = lax.axis_index("tok")
    head_index = lax.axis_index("head")
    prompts = lengths.shape[0]
    prompt_ends = jnp.cumsum(lengths)
    starts = prompt_ends - lengths
    global_index = tok_index * shard_rows + jnp.arange(shard_rows, dtype=jnp.int32)
    positions = global_index - lookup_table(segment_ids, starts)
    widened = tokens.astype(jnp.float32)
    normed = (
        widened
        * lax.rsqrt(jnp.mean(widened * widened, axis=1, keepdims=True) + 1e-06)
        * norm_gain.astype(jnp.float32)
    ).astype(jnp.bfloat16)

    def add_rows(piece):
        return jnp.dot(normed, piece, preferred_element_type=jnp.float32)

    queries = add_rows(lax.all_gather(w_query, "tok", axis=0, tiled=True))
    queries = rotate(queries.reshape(shard_rows, heads_here, HD), positions).astype(jnp.bfloat16)
    keyval = add_rows(lax.all_gather(w_keyval, "tok", axis=0, tiled=True))
    rotated = rotate(keyval[:, None, :HD], positions)[:, 0]
    pairs = jnp.concatenate([rotated, keyval[:, HD:]], axis=1).astype(jnp.bfloat16)
    rim_shards = -(-WINDOW // shard_rows)
    rim_pairs = []
    rim_segments = []
    for distance in range(rim_shards, 0, -1):
        got_pairs, got_segments = shifted((pairs, segment_ids), "tok", distance)
        rim_pairs.append(got_pairs)
        rim_segments.append(got_segments)
    all_pairs = jnp.concatenate(rim_pairs + [pairs], axis=0)
    key_segments = jnp.concatenate(rim_segments + [segment_ids], axis=0)
    key_index = (tok_index - rim_shards) * shard_rows + jnp.arange(
        (rim_shards + 1) * shard_rows, dtype=jnp.int32
    )
    score_scale = 1.0 / math.sqrt(HD)
    outputs = []
    for head_slot in range(heads_here):
        query_head = queries[:, head_slot, :]
        scores = (
            jnp.einsum(
                "qd,kd->qk", query_head, all_pairs[:, :HD], preferred_element_type=jnp.float32
            )
            * score_scale
        )
        allowed = (key_segments[None, :] == segment_ids[:, None]) & (
            key_index[None, :] <= global_index[:, None]
        )
        allowed = (
            allowed
            & (key_index[None, :] > global_index[:, None] - WINDOW)
            & (key_index[None, :] >= 0)
        )
        scores = jnp.where(allowed, scores, -jnp.inf)
        largest = jnp.max(scores, axis=1, keepdims=True)
        weights = jnp.exp(scores - largest)
        total = jnp.sum(weights, axis=1, keepdims=True)
        probs = weights.astype(jnp.bfloat16)
        summed = jnp.dot(probs, all_pairs[:, HD:], preferred_element_type=jnp.float32)
        outputs.append((summed / total).astype(jnp.bfloat16))
    attention = jnp.concatenate(outputs, axis=1)
    quarter_cols = tokens.shape[1] // lax.axis_size("head")
    residual = lax.dynamic_slice_in_dim(tokens, head_index * quarter_cols, quarter_cols, 1).astype(
        jnp.float32
    )
    partial_out = jnp.dot(
        attention,
        lax.all_gather(w_out, "tok", axis=1, tiled=True),
        preferred_element_type=jnp.float32,
    )
    head_total = lax.psum_scatter(
        partial_out.astype(jnp.bfloat16), "head", scatter_dimension=1, tiled=True
    ).astype(jnp.float32)
    mixed = (residual + head_total).astype(jnp.bfloat16)
    slots_here = WINDOW // devices
    first_segment = jnp.sum((prompt_ends <= tok_index * shard_rows).astype(jnp.int32))
    slot_index = jnp.arange(WINDOW, dtype=jnp.int32)
    prompt_index = jnp.arange(prompts, dtype=jnp.int32)
    outgoing = []
    for local_seg in range(2):
        prompt_here = first_segment + local_seg
        matches = prompt_index == prompt_here
        prompt_size = jnp.sum(jnp.where(matches, lengths, 0))
        prompt_start = jnp.sum(jnp.where(matches, starts, 0))
        lowest = prompt_size - WINDOW
        places = lowest + jnp.mod(slot_index - lowest, WINDOW)
        local_rows = prompt_start + places - tok_index * shard_rows
        usable = (
            (prompt_here < prompts) & (places >= 0) & (local_rows >= 0) & (local_rows < shard_rows)
        )
        fetched = jnp.take(pairs, jnp.clip(local_rows, 0, shard_rows - 1), axis=0)
        kept = jnp.where(usable[:, None], fetched, jnp.zeros_like(fetched))
        outgoing.append(kept.reshape(devices, slots_here * 2 * HD))
    incoming = lax.all_to_all(jnp.stack(outgoing), "tok", split_axis=1, concat_axis=1, tiled=True)
    source_rows = jnp.arange(devices, dtype=jnp.int32) * shard_rows
    source_first = jnp.sum((prompt_ends[None, :] <= source_rows[:, None]).astype(jnp.int32), axis=1)
    owners = jnp.stack([source_first, source_first + 1]).reshape(-1)
    chooser = (owners[None, :] == prompt_index[:, None]).astype(jnp.bfloat16)
    slot_table = jnp.dot(
        chooser,
        incoming.reshape(2 * devices, slots_here * 2 * HD),
        preferred_element_type=jnp.float32,
    ).astype(jnp.bfloat16)
    member_pick = (member_prompt[:, None] == prompt_index[None, :]).astype(jnp.bfloat16)
    cycle_cache = jnp.dot(member_pick, slot_table, preferred_element_type=jnp.float32).astype(
        jnp.bfloat16
    )
    cycle_cache = cycle_cache.reshape(member_prompt.shape[0], slots_here, 2 * HD)
    return (mixed, cycle_cache)


def solution(mesh):
    return jax.shard_map(
        per_device,
        mesh=mesh,
        in_specs=(
            P("tok", None),
            P(),
            P("tok", "head"),
            P("tok", None),
            P("head", "tok"),
            P("tok"),
            P(),
            P("head"),
        ),
        out_specs=(P("tok", "head"), P("head", "tok", None)),
        check_vma=False,
    )
```

profile of v0, /device:TPU:8, one launch (start us, length us, event | category | flops | bytes accessed | tf_op | source)
XLA Modules:
  0.0 275.0 jit_solution(13498664107108925658)
XLA Ops:
  10.7 57.2 %all-gather.1 = bf16[128,12,256]{2,1,0:T(8,128)(2,1)S(1)} all-gather(bf16[1,12,256]{2,1,0:T(8,128)(2,1)} %bitcast.50), channel_id=1, replica_groups=mesh['tok'=128,'head'=4] {'tok'}, dimensions={0}, use_global_device_ids=true | all-gather | bytes 792576 | tf_op jit(solution)/shard_map/all_gather | solution.py:62
  71.7 6.0 %collective-permute-start.8 = (bf16[128,256]{0,1:T(8,128)(2,1)S(1)}, bf16[128,256]{0,1:T(8,128)(2,1)S(1)}, u32[]{:S(2)}, u32[]{:S(2)}) collective-permute-start(bf16[128,256]{0,1:T(8,128)(2,1)S(1)} %pad_maximum_fusion.1), channel_id=1, source_target_pairs={{0,32},{4,36},{8,40},{12,44},{16,48},{20,52},{24,56},{28,60},{32,6... | collective-permute-start | bytes 196616 | tf_op jit(solution)/shard_map/ppermute | solution.py:14
  77.8 3.4 %collective-permute-start.9 = (bf16[128,256]{0,1:T(8,128)(2,1)S(1)}, bf16[128,256]{0,1:T(8,128)(2,1)S(1)}, u32[]{:S(2)}, u32[]{:S(2)}) collective-permute-start(bf16[128,256]{0,1:T(8,128)(2,1)S(1)} %pad_maximum_fusion.1), channel_id=1, source_target_pairs={{0,28},{4,32},{8,36},{12,40},{16,44},{20,48},{24,52},{28,56},{32,6... | collective-permute-start | bytes 196616 | tf_op jit(solution)/shard_map/ppermute | solution.py:14
  81.2 4.8 %collective-permute-start.10 = (bf16[128,256]{0,1:T(8,128)(2,1)S(1)}, bf16[128,256]{0,1:T(8,128)(2,1)S(1)}, u32[]{:S(2)}, u32[]{:S(2)}) collective-permute-start(bf16[128,256]{0,1:T(8,128)(2,1)S(1)} %pad_maximum_fusion.1), channel_id=1, source_target_pairs={{0,24},{4,28},{8,32},{12,36},{16,40},{20,44},{24,48},{28,52},{32,5... | collective-permute-start | bytes 196616 | tf_op jit(solution)/shard_map/ppermute | solution.py:14
  86.0 3.2 %collective-permute-start.11 = (bf16[128,256]{0,1:T(8,128)(2,1)S(1)}, bf16[128,256]{0,1:T(8,128)(2,1)S(1)}, u32[]{:S(2)}, u32[]{:S(2)}) collective-permute-start(bf16[128,256]{0,1:T(8,128)(2,1)S(1)} %pad_maximum_fusion.1), channel_id=1, source_target_pairs={{0,20},{4,24},{8,28},{12,32},{16,36},{20,40},{24,44},{28,48},{32,5... | collective-permute-start | bytes 196616 | tf_op jit(solution)/shard_map/ppermute | solution.py:14
  89.2 5.1 %collective-permute-start = (s32[128]{0:T(128)S(1)}, s32[128]{0:T(128)S(1)}, u32[]{:S(2)}, u32[]{:S(2)}) collective-permute-start(s32[128]{0:T(128)S(1)} %copy-done.4), channel_id=1, source_target_pairs={{0,32},{4,36},{8,40},{12,44},{16,48},{20,52},{24,56},{28,60},{32,6... | collective-permute-start | bytes 1544 | tf_op jit(solution)/shard_map/ppermute | solution.py:14
  97.6 3.9 %gather_fusion = bf16[1024,256]{1,0:T(8,128)(2,1)S(1)} fusion(bf16[128,256]{1,0:T(8,128)(2,1)S(1)} %copy.46, s32[1024]{0:T(1024)S(1)} %get-tuple-element.27), kind=kCustom, calls=%fused_computation.clone | custom fusion | bytes 1052672 | tf_op jit(solution)/shard_map/jit(_take)/gather | solution.py:132
  104.8 3.9 %gather_fusion.1 = bf16[1024,256]{1,0:T(8,128)(2,1)S(1)} fusion(bf16[128,256]{1,0:T(8,128)(2,1)S(1)} %copy.46, s32[1024]{0:T(1024)S(1)} %get-tuple-element.28), kind=kCustom, calls=%fused_computation.1.clone | custom fusion | bytes 1052672 | tf_op jit(solution)/shard_map/jit(_take)/gather | solution.py:132
  109.3 3.2 %pad_maximum_fusion = bf16[2,128,2048]{2,0,1:T(2,128)(2,1)} fusion(bf16[1,128,2048]{2,0,1:T(2,128)(2,1)S(1)} %stack_reshape.9, bf16[1,128,2048]{2,0,1:T(2,128)(2,1)S(1)} %stack_reshape.8), kind=kLoop, calls=%fused_computation.17 | loop fusion | flops 2097152 | bytes 2097152 | tf_op jit(solution)/shard_map/stack | solution.py:135
  112.6 9.8 %all-to-all-start = ((bf16[2,128,2048]{2,0,1:T(2,128)(2,1)}), bf16[2,128,2048]{2,0,1:T(2,128)(2,1)S(1)}, u32[]{:S(2)}, u32[]{:S(2)}) async-start(bf16[2,128,2048]{2,0,1:T(2,128)(2,1)} %pad_maximum_fusion), calls=%async_computation | async-start | bytes 2097152 | tf_op jit(solution)/shard_map/all_to_all | solution.py:135
  123.4 6.1 %collective-permute-start.1 = (s32[128]{0:T(128)S(1)}, s32[128]{0:T(128)S(1)}, u32[]{:S(2)}, u32[]{:S(2)}) collective-permute-start(s32[128]{0:T(128)S(1)} %copy-done.4), channel_id=1, source_target_pairs={{0,28},{4,32},{8,36},{12,40},{16,44},{20,48},{24,52},{28,56},{32,6... | collective-permute-start | bytes 1544 | tf_op jit(solution)/shard_map/ppermute | solution.py:14
  129.5 14.7 %collective-permute-done.1 = s32[128]{0:T(128)S(1)} collective-permute-done((s32[128]{0:T(128)S(1)}, s32[128]{0:T(128)S(1)}, u32[]{:S(2)}, u32[]{:S(2)}) %collective-permute-start.1) | collective-permute-done | bytes 544 | tf_op jit(solution)/shard_map/ppermute | solution.py:14
  144.3 6.8 %collective-permute-start.2 = (s32[128]{0:T(128)S(1)}, s32[128]{0:T(128)S(1)}, u32[]{:S(2)}, u32[]{:S(2)}) collective-permute-start(s32[128]{0:T(128)S(1)} %copy-done.4), channel_id=1, source_target_pairs={{0,24},{4,28},{8,32},{12,36},{16,40},{20,44},{24,48},{28,52},{32,5... | collective-permute-start | bytes 1544 | tf_op jit(solution)/shard_map/ppermute | solution.py:14
  152.4 3.9 %collective-permute-start.3 = (s32[128]{0:T(128)S(1)}, s32[128]{0:T(128)S(1)}, u32[]{:S(2)}, u32[]{:S(2)}) collective-permute-start(s32[128]{0:T(128)S(1)} %copy-done.4), channel_id=1, source_target_pairs={{0,20},{4,24},{8,28},{12,32},{16,36},{20,40},{24,44},{28,48},{32,5... | collective-permute-start | bytes 1544 | tf_op jit(solution)/shard_map/ppermute | solution.py:14
  157.6 6.5 %collective-permute-start.4 = (s32[128]{0:T(128)S(1)}, s32[128]{0:T(128)S(1)}, u32[]{:S(2)}, u32[]{:S(2)}) collective-permute-start(s32[128]{0:T(128)S(1)} %copy-done.4), channel_id=1, source_target_pairs={{0,16},{4,20},{8,24},{12,28},{16,32},{20,36},{24,40},{28,44},{32,4... | collective-permute-start | bytes 1544 | tf_op jit(solution)/shard_map/ppermute | solution.py:14
  165.4 3.5 %collective-permute-start.5 = (s32[128]{0:T(128)S(1)}, s32[128]{0:T(128)S(1)}, u32[]{:S(2)}, u32[]{:S(2)}) collective-permute-start(s32[128]{0:T(128)S(1)} %copy-done.4), channel_id=1, source_target_pairs={{0,12},{4,16},{8,20},{12,24},{16,28},{20,32},{24,36},{28,40},{32,4... | collective-permute-start | bytes 1544 | tf_op jit(solution)/shard_map/ppermute | solution.py:14
  170.2 6.8 %collective-permute-start.6 = (s32[128]{0:T(128)S(1)}, s32[128]{0:T(128)S(1)}, u32[]{:S(2)}, u32[]{:S(2)}) collective-permute-start(s32[128]{0:T(128)S(1)} %copy-done.4), channel_id=1, source_target_pairs={{0,8},{4,12},{8,16},{12,20},{16,24},{20,28},{24,32},{28,36},{32,40... | collective-permute-start | bytes 1544 | tf_op jit(solution)/shard_map/ppermute | solution.py:14
  178.2 2.4 collective-permute-start.7
  180.6 2.5 collective-permute-done.7
  183.1 7.5 %collective-permute-start.12 = (bf16[128,256]{0,1:T(8,128)(2,1)S(1)}, bf16[128,256]{0,1:T(8,128)(2,1)S(1)}, u32[]{:S(2)}, u32[]{:S(2)}) collective-permute-start(bf16[128,256]{0,1:T(8,128)(2,1)S(1)} %pad_maximum_fusion.1), channel_id=1, source_target_pairs={{0,16},{4,20},{8,24},{12,28},{16,32},{20,36},{24,40},{28,44},{32,4... | collective-permute-start | bytes 196616 | tf_op jit(solution)/shard_map/ppermute | solution.py:14
  190.6 3.2 %collective-permute-start.13 = (bf16[128,256]{0,1:T(8,128)(2,1)S(1)}, bf16[128,256]{0,1:T(8,128)(2,1)S(1)}, u32[]{:S(2)}, u32[]{:S(2)}) collective-permute-start(bf16[128,256]{0,1:T(8,128)(2,1)S(1)} %pad_maximum_fusion.1), channel_id=1, source_target_pairs={{0,12},{4,16},{8,20},{12,24},{16,28},{20,32},{24,36},{28,40},{32,4... | collective-permute-start | bytes 196616 | tf_op jit(solution)/shard_map/ppermute | solution.py:14
  194.4 5.4 %collective-permute-start.14 = (bf16[128,256]{0,1:T(8,128)(2,1)S(1)}, bf16[128,256]{0,1:T(8,128)(2,1)S(1)}, u32[]{:S(2)}, u32[]{:S(2)}) collective-permute-start(bf16[128,256]{0,1:T(8,128)(2,1)S(1)} %pad_maximum_fusion.1), channel_id=1, source_target_pairs={{0,8},{4,12},{8,16},{12,20},{16,24},{20,28},{24,32},{28,36},{32,40... | collective-permute-start | bytes 196616 | tf_op jit(solution)/shard_map/ppermute | solution.py:14
  200.5 2.8 %collective-permute-start.15 = (bf16[128,256]{0,1:T(8,128)(2,1)S(1)}, bf16[128,256]{0,1:T(8,128)(2,1)S(1)}, u32[]{:S(2)}, u32[]{:S(2)}) collective-permute-start(bf16[128,256]{0,1:T(8,128)(2,1)S(1)} %pad_maximum_fusion.1), channel_id=1, source_target_pairs={{0,4},{4,8},{8,12},{12,16},{16,20},{20,24},{24,28},{28,32},{32,36}... | collective-permute-start | bytes 196616 | tf_op jit(solution)/shard_map/ppermute | solution.py:14
  227.0 39.8 %reduce-scatter.4.cloned.1.call-done = bf16[384,128]{1,0:T(8,128)(2,1)} async-done(((bf16[1536,128]{1,0:T(8,128)(2,1)}), bf16[384,128]{1,0:T(8,128)(2,1)}) %reduce-scatter.4.cloned.1.call-update) | async-done | bytes 98320
  (106 shorter events, 45.8 us)
Async XLA Ops:
  7.2 200.6 %all-gather.6.cloned.1.call-start = ((), (), s32[]{:S(2)}) async-start(), calls=%async_computation.2 | async-start | bytes 1585152 | tf_op jit(solution)/shard_map/all_gather | solution.py:60
  67.8 1.0 copy-start
  67.8 2.1 copy-start.2
  67.9 3.5 %copy-start.4 = (s32[128]{0:T(128)S(1)}, s32[128]{0:T(128)}, u32[]{:S(2)}) copy-start(s32[128]{0:T(128)} %param.15) | copy-start | bytes 1540
  71.7 118.9 %collective-permute-start.8 = (bf16[128,256]{0,1:T(8,128)(2,1)S(1)}, bf16[128,256]{0,1:T(8,128)(2,1)S(1)}, u32[]{:S(2)}, u32[]{:S(2)}) collective-permute-start(bf16[128,256]{0,1:T(8,128)(2,1)S(1)} %pad_maximum_fusion.1), channel_id=1, source_target_pairs={{0,32},{4,36},{8,40},{12,44},{16,48},{20,52},{24,56},{28,60},{32,6... | collective-permute-start | bytes 196616 | tf_op jit(solution)/shard_map/ppermute | solution.py:14
  77.8 116.7 %collective-permute-start.9 = (bf16[128,256]{0,1:T(8,128)(2,1)S(1)}, bf16[128,256]{0,1:T(8,128)(2,1)S(1)}, u32[]{:S(2)}, u32[]{:S(2)}) collective-permute-start(bf16[128,256]{0,1:T(8,128)(2,1)S(1)} %pad_maximum_fusion.1), channel_id=1, source_target_pairs={{0,28},{4,32},{8,36},{12,40},{16,44},{20,48},{24,52},{28,56},{32,6... | collective-permute-start | bytes 196616 | tf_op jit(solution)/shard_map/ppermute | solution.py:14
  81.2 119.3 %collective-permute-start.10 = (bf16[128,256]{0,1:T(8,128)(2,1)S(1)}, bf16[128,256]{0,1:T(8,128)(2,1)S(1)}, u32[]{:S(2)}, u32[]{:S(2)}) collective-permute-start(bf16[128,256]{0,1:T(8,128)(2,1)S(1)} %pad_maximum_fusion.1), channel_id=1, source_target_pairs={{0,24},{4,28},{8,32},{12,36},{16,40},{20,44},{24,48},{28,52},{32,5... | collective-permute-start | bytes 196616 | tf_op jit(solution)/shard_map/ppermute | solution.py:14
  86.0 117.9 %collective-permute-start.11 = (bf16[128,256]{0,1:T(8,128)(2,1)S(1)}, bf16[128,256]{0,1:T(8,128)(2,1)S(1)}, u32[]{:S(2)}, u32[]{:S(2)}) collective-permute-start(bf16[128,256]{0,1:T(8,128)(2,1)S(1)} %pad_maximum_fusion.1), channel_id=1, source_target_pairs={{0,20},{4,24},{8,28},{12,32},{16,36},{20,40},{24,44},{28,48},{32,5... | collective-permute-start | bytes 196616 | tf_op jit(solution)/shard_map/ppermute | solution.py:14
  89.2 34.2 %collective-permute-start = (s32[128]{0:T(128)S(1)}, s32[128]{0:T(128)S(1)}, u32[]{:S(2)}, u32[]{:S(2)}) collective-permute-start(s32[128]{0:T(128)S(1)} %copy-done.4), channel_id=1, source_target_pairs={{0,32},{4,36},{8,40},{12,44},{16,48},{20,52},{24,56},{28,60},{32,6... | collective-permute-start | bytes 1544 | tf_op jit(solution)/shard_map/ppermute | solution.py:14
  112.6 112.6 %all-to-all-start = ((bf16[2,128,2048]{2,0,1:T(2,128)(2,1)}), bf16[2,128,2048]{2,0,1:T(2,128)(2,1)S(1)}, u32[]{:S(2)}, u32[]{:S(2)}) async-start(bf16[2,128,2048]{2,0,1:T(2,128)(2,1)} %pad_maximum_fusion), calls=%async_computation | async-start | bytes 2097152 | tf_op jit(solution)/shard_map/all_to_all | solution.py:135
  122.4 92.1 %all-gather.8.cloned.1.call-start = ((), (), s32[]{:S(2)}) async-start(), calls=%async_computation.3 | async-start | bytes 1585152 | tf_op jit(solution)/shard_map/all_gather | solution.py:109
  123.1 143.7 %reduce-scatter.4.cloned.1.call-start = ((), (), s32[]{:S(2)}) async-start(), calls=%async_computation.4 | async-start | bytes 491520
  123.4 20.9 %collective-permute-start.1 = (s32[128]{0:T(128)S(1)}, s32[128]{0:T(128)S(1)}, u32[]{:S(2)}, u32[]{:S(2)}) collective-permute-start(s32[128]{0:T(128)S(1)} %copy-done.4), channel_id=1, source_target_pairs={{0,28},{4,32},{8,36},{12,40},{16,44},{20,48},{24,52},{28,56},{32,6... | collective-permute-start | bytes 1544 | tf_op jit(solution)/shard_map/ppermute | solution.py:14
  144.3 8.1 %collective-permute-start.2 = (s32[128]{0:T(128)S(1)}, s32[128]{0:T(128)S(1)}, u32[]{:S(2)}, u32[]{:S(2)}) collective-permute-start(s32[128]{0:T(128)S(1)} %copy-done.4), channel_id=1, source_target_pairs={{0,24},{4,28},{8,32},{12,36},{16,40},{20,44},{24,48},{28,52},{32,5... | collective-permute-start | bytes 1544 | tf_op jit(solution)/shard_map/ppermute | solution.py:14
  152.4 5.2 %collective-permute-start.3 = (s32[128]{0:T(128)S(1)}, s32[128]{0:T(128)S(1)}, u32[]{:S(2)}, u32[]{:S(2)}) collective-permute-start(s32[128]{0:T(128)S(1)} %copy-done.4), channel_id=1, source_target_pairs={{0,20},{4,24},{8,28},{12,32},{16,36},{20,40},{24,44},{28,48},{32,5... | collective-permute-start | bytes 1544 | tf_op jit(solution)/shard_map/ppermute | solution.py:14
  157.6 7.8 %collective-permute-start.4 = (s32[128]{0:T(128)S(1)}, s32[128]{0:T(128)S(1)}, u32[]{:S(2)}, u32[]{:S(2)}) collective-permute-start(s32[128]{0:T(128)S(1)} %copy-done.4), channel_id=1, source_target_pairs={{0,16},{4,20},{8,24},{12,28},{16,32},{20,36},{24,40},{28,44},{32,4... | collective-permute-start | bytes 1544 | tf_op jit(solution)/shard_map/ppermute | solution.py:14
  165.4 4.8 %collective-permute-start.5 = (s32[128]{0:T(128)S(1)}, s32[128]{0:T(128)S(1)}, u32[]{:S(2)}, u32[]{:S(2)}) collective-permute-start(s32[128]{0:T(128)S(1)} %copy-done.4), channel_id=1, source_target_pairs={{0,12},{4,16},{8,20},{12,24},{16,28},{20,32},{24,36},{28,40},{32,4... | collective-permute-start | bytes 1544 | tf_op jit(solution)/shard_map/ppermute | solution.py:14
  170.2 8.1 %collective-permute-start.6 = (s32[128]{0:T(128)S(1)}, s32[128]{0:T(128)S(1)}, u32[]{:S(2)}, u32[]{:S(2)}) collective-permute-start(s32[128]{0:T(128)S(1)} %copy-done.4), channel_id=1, source_target_pairs={{0,8},{4,12},{8,16},{12,20},{16,24},{20,28},{24,32},{28,36},{32,40... | collective-permute-start | bytes 1544 | tf_op jit(solution)/shard_map/ppermute | solution.py:14
  178.2 4.9 %collective-permute-start.7 = (s32[128]{0:T(128)S(1)}, s32[128]{0:T(128)S(1)}, u32[]{:S(2)}, u32[]{:S(2)}) collective-permute-start(s32[128]{0:T(128)S(1)} %copy-done.4), channel_id=1, source_target_pairs={{0,4},{4,8},{8,12},{12,16},{16,20},{20,24},{24,28},{28,32},{32,36}... | collective-permute-start | bytes 1544 | tf_op jit(solution)/shard_map/ppermute | solution.py:14
  183.1 21.4 %collective-permute-start.12 = (bf16[128,256]{0,1:T(8,128)(2,1)S(1)}, bf16[128,256]{0,1:T(8,128)(2,1)S(1)}, u32[]{:S(2)}, u32[]{:S(2)}) collective-permute-start(bf16[128,256]{0,1:T(8,128)(2,1)S(1)} %pad_maximum_fusion.1), channel_id=1, source_target_pairs={{0,16},{4,20},{8,24},{12,28},{16,32},{20,36},{24,40},{28,44},{32,4... | collective-permute-start | bytes 196616 | tf_op jit(solution)/shard_map/ppermute | solution.py:14
  190.6 14.6 %collective-permute-start.13 = (bf16[128,256]{0,1:T(8,128)(2,1)S(1)}, bf16[128,256]{0,1:T(8,128)(2,1)S(1)}, u32[]{:S(2)}, u32[]{:S(2)}) collective-permute-start(bf16[128,256]{0,1:T(8,128)(2,1)S(1)} %pad_maximum_fusion.1), channel_id=1, source_target_pairs={{0,12},{4,16},{8,20},{12,24},{16,28},{20,32},{24,36},{28,40},{32,4... | collective-permute-start | bytes 196616 | tf_op jit(solution)/shard_map/ppermute | solution.py:14
  194.4 11.4 %collective-permute-start.14 = (bf16[128,256]{0,1:T(8,128)(2,1)S(1)}, bf16[128,256]{0,1:T(8,128)(2,1)S(1)}, u32[]{:S(2)}, u32[]{:S(2)}) collective-permute-start(bf16[128,256]{0,1:T(8,128)(2,1)S(1)} %pad_maximum_fusion.1), channel_id=1, source_target_pairs={{0,8},{4,12},{8,16},{12,20},{16,24},{20,28},{24,32},{28,36},{32,40... | collective-permute-start | bytes 196616 | tf_op jit(solution)/shard_map/ppermute | solution.py:14
  200.5 6.0 %collective-permute-start.15 = (bf16[128,256]{0,1:T(8,128)(2,1)S(1)}, bf16[128,256]{0,1:T(8,128)(2,1)S(1)}, u32[]{:S(2)}, u32[]{:S(2)}) collective-permute-start(bf16[128,256]{0,1:T(8,128)(2,1)S(1)} %pad_maximum_fusion.1), channel_id=1, source_target_pairs={{0,4},{4,8},{8,12},{12,16},{16,20},{20,24},{24,28},{28,32},{32,36}... | collective-permute-start | bytes 196616 | tf_op jit(solution)/shard_map/ppermute | solution.py:14
  219.4 1.5 copy-start.1
  (1 other events, 0.7 us)
Sparse Core Ops, SparseCore 0:
  11.2 89.9 all-gather.5
  126.4 84.7 all-gather.7
  225.2 41.6 reduce-scatter.3
where the time goes:
time: 276 us; the launch traced here: 275 us
  starting transfers between devices  87.2 us (32%)
  waiting for transfers between devices  64.8 us (23%)
  blocking collectives  57.2 us (21%)
  local copies, waits for them, and re-layouts  22.6 us (8%)
  between operations  16.8 us (6%)
  other arithmetic  15.6 us (6%)
  matrix products  10.9 us (4%)
    ppermute x16, starting transfers between devices, shifted(): return lax.ppermute(block, axis, route)  77.3 us
    all_gather x1, blocking collectives, per_device(): keyval = add_rows(lax.all_gather(w_keyval, 'tok', axis=0, tiled=True))  57.2 us
    unnamed x4, waiting for transfers between devices  41.2 us
    ppermute x16, waiting for transfers between devices, shifted(): return lax.ppermute(block, axis, route)  23.6 us
    unnamed x32, local copies, waits for them, and re-layouts  13 us
    all_to_all x1, starting transfers between devices, per_device(): lax.all_to_all(jnp.stack(outgoing), 'tok', split_axis=1, concat_axis=1, t...  9.78 us
    gather x2, local copies, waits for them, and re-layouts, per_device(): fetched = jnp.take(pairs, jnp.clip(local_rows, 0, shard_rows - 1), axis=0)  7.88 us
  transfers between devices with their start and end apart: 20, of which 8 were waited for; matrix products, arithmetic and copies ran while one was open for 17% of the time, Pallas kernels for 0%

commit v1 on v0

--- a/solution.py
+++ b/solution.py
@@ -59,7 +59,11 @@
 
     queries = add_rows(lax.all_gather(w_query, "tok", axis=0, tiled=True))
     queries = rotate(queries.reshape(shard_rows, heads_here, HD), positions).astype(jnp.bfloat16)
-    keyval = add_rows(lax.all_gather(w_keyval, "tok", axis=0, tiled=True))
+    keyval = add_rows(
+        jnp.concatenate(
+            lax.all_to_all(jnp.stack([w_keyval] * lax.axis_size("tok")), "tok", 0, 0), axis=0
+        )
+    )
     rotated = rotate(keyval[:, None, :HD], positions)[:, 0]
     pairs = jnp.concatenate([rotated, keyval[:, HD:]], axis=1).astype(jnp.bfloat16)
     rim_shards = -(-WINDOW // shard_rows)

time: 276 us -> 249 us (0.902)
  the two profiles are of different devices: /device:TPU:8 before, /device:TPU:16 now
where the time goes in v1:
time: 249 us; the launch traced here: 248 us
  waiting for transfers between devices  102 us (41%)
  starting transfers between devices  88.9 us (36%)
  local copies, waits for them, and re-layouts  21 us (8%)
  between operations  17 us (7%)
  other arithmetic  12.3 us (5%)
  matrix products  6.58 us (3%)
    ppermute x16, starting transfers between devices, shifted(): return lax.ppermute(block, axis, route)  65 us
    all_gather x1, waiting for transfers between devices, per_device(): lax.all_gather(w_out, 'tok', axis=1, tiled=True)  49.3 us
    unnamed x4, waiting for transfers between devices  25 us
    ppermute x16, waiting for transfers between devices, shifted(): return lax.ppermute(block, axis, route)  19.7 us
    all_to_all x1, starting transfers between devices, per_device(): lax.all_to_all(jnp.stack([w_keyval] * lax.axis_size('tok')), 'tok', 0, 0)  15.7 us
    unnamed x41, local copies, waits for them, and re-layouts  10.2 us
    all_to_all x1, starting transfers between devices, per_device(): lax.all_to_all(jnp.stack(outgoing), 'tok', split_axis=1, concat_axis=1, t...  8.12 us
    gather x2, local copies, waits for them, and re-layouts, per_device(): fetched = jnp.take(pairs, jnp.clip(local_rows, 0, shard_rows - 1), axis=0)  7.88 us
  transfers between devices with their start and end apart: 21, of which 8 were waited for; matrix products, arithmetic and copies ran while one was open for 15% of the time, Pallas kernels for 0%

profile of v1, /device:TPU:16, one launch (start us, length us, event | category | flops | bytes accessed | tf_op | source)
XLA Modules:
  0.0 247.8 jit_solution(16428527446908678231)
XLA Ops:
  7.9 5.9 %collective-permute-start = (s32[128]{0:T(128)}, s32[128]{0:T(128)S(1)}, u32[]{:S(2)}, u32[]{:S(2)}) collective-permute-start(s32[128]{0:T(128)} %param.15), channel_id=1, source_target_pairs={{0,32},{4,36},{8,40},{12,44},{16,48},{20,52},{24,56},{28,60},{32,6... | collective-permute-start | bytes 1544 | tf_op jit(solution)/shard_map/ppermute | solution.py:14
  13.8 3.8 %collective-permute-start.1 = (s32[128]{0:T(128)}, s32[128]{0:T(128)S(1)}, u32[]{:S(2)}, u32[]{:S(2)}) collective-permute-start(s32[128]{0:T(128)} %param.15), channel_id=1, source_target_pairs={{0,28},{4,32},{8,36},{12,40},{16,44},{20,48},{24,52},{28,56},{32,6... | collective-permute-start | bytes 1544 | tf_op jit(solution)/shard_map/ppermute | solution.py:14
  17.6 6.7 %collective-permute-start.2 = (s32[128]{0:T(128)}, s32[128]{0:T(128)S(1)}, u32[]{:S(2)}, u32[]{:S(2)}) collective-permute-start(s32[128]{0:T(128)} %param.15), channel_id=1, source_target_pairs={{0,24},{4,28},{8,32},{12,36},{16,40},{20,44},{24,48},{28,52},{32,5... | collective-permute-start | bytes 1544 | tf_op jit(solution)/shard_map/ppermute | solution.py:14
  24.3 3.1 %collective-permute-start.3 = (s32[128]{0:T(128)}, s32[128]{0:T(128)S(1)}, u32[]{:S(2)}, u32[]{:S(2)}) collective-permute-start(s32[128]{0:T(128)} %param.15), channel_id=1, source_target_pairs={{0,20},{4,24},{8,28},{12,32},{16,36},{20,40},{24,44},{28,48},{32,5... | collective-permute-start | bytes 1544 | tf_op jit(solution)/shard_map/ppermute | solution.py:14
  27.5 4.5 %collective-permute-start.4 = (s32[128]{0:T(128)}, s32[128]{0:T(128)S(1)}, u32[]{:S(2)}, u32[]{:S(2)}) collective-permute-start(s32[128]{0:T(128)} %param.15), channel_id=1, source_target_pairs={{0,16},{4,20},{8,24},{12,28},{16,32},{20,36},{24,40},{28,44},{32,4... | collective-permute-start | bytes 1544 | tf_op jit(solution)/shard_map/ppermute | solution.py:14
  33.7 15.7 %all-to-all-start = ((bf16[128,12,256]{2,1,0:T(8,128)(2,1)}), bf16[128,12,256]{2,1,0:T(8,128)(2,1)S(1)}, u32[]{:S(2)}, u32[]{:S(2)}) async-start(bf16[128,12,256]{2,1,0:T(8,128)(2,1)} %stack.8), calls=%async_computation | async-start | bytes 2097152 | tf_op jit(solution)/shard_map/all_to_all | solution.py:64
  59.6 3.1 %collective-permute-start.5 = (s32[128]{0:T(128)S(1)}, s32[128]{0:T(128)S(1)}, u32[]{:S(2)}, u32[]{:S(2)}) collective-permute-start(s32[128]{0:T(128)S(1)} %copy-done.9), channel_id=1, source_target_pairs={{0,12},{4,16},{8,20},{12,24},{16,28},{20,32},{24,36},{28,40},{32,4... | collective-permute-start | bytes 1544 | tf_op jit(solution)/shard_map/ppermute | solution.py:14
  62.7 4.6 %collective-permute-start.6 = (s32[128]{0:T(128)S(1)}, s32[128]{0:T(128)S(1)}, u32[]{:S(2)}, u32[]{:S(2)}) collective-permute-start(s32[128]{0:T(128)S(1)} %copy-done.9), channel_id=1, source_target_pairs={{0,8},{4,12},{8,16},{12,20},{16,24},{20,28},{24,32},{28,36},{32,40... | collective-permute-start | bytes 1544 | tf_op jit(solution)/shard_map/ppermute | solution.py:14
  72.4 7.9 %all-to-all-done = bf16[128,12,256]{2,1,0:T(8,128)(2,1)S(1)} async-done(((bf16[128,12,256]{2,1,0:T(8,128)(2,1)}), bf16[128,12,256]{2,1,0:T(8,128)(2,1)S(1)}, u32[]{:S(2)}, u32[]{:S(2)}) %all-to-all-start) | async-done | bytes 786464 | tf_op jit(solution)/shard_map/all_to_all | solution.py:64
  81.3 4.2 %collective-permute-start.8 = (bf16[128,256]{0,1:T(8,128)(2,1)S(1)}, bf16[128,256]{0,1:T(8,128)(2,1)}, u32[]{:S(2)}, u32[]{:S(2)}) collective-permute-start(bf16[128,256]{0,1:T(8,128)(2,1)S(1)} %pad_maximum_fusion.1), channel_id=1, source_target_pairs={{0,32},{4,36},{8,40},{12,44},{16,48},{20,52},{24,56},{28,60},{32,6... | collective-permute-start | bytes 196616 | tf_op jit(solution)/shard_map/ppermute | solution.py:14
  85.5 4.1 %collective-permute-start.9 = (bf16[128,256]{0,1:T(8,128)(2,1)S(1)}, bf16[128,256]{0,1:T(8,128)(2,1)S(1)}, u32[]{:S(2)}, u32[]{:S(2)}) collective-permute-start(bf16[128,256]{0,1:T(8,128)(2,1)S(1)} %pad_maximum_fusion.1), channel_id=1, source_target_pairs={{0,28},{4,32},{8,36},{12,40},{16,44},{20,48},{24,52},{28,56},{32,6... | collective-permute-start | bytes 196616 | tf_op jit(solution)/shard_map/ppermute | solution.py:14
  89.5 3.7 %collective-permute-start.10 = (bf16[128,256]{0,1:T(8,128)(2,1)S(1)}, bf16[128,256]{0,1:T(8,128)(2,1)S(1)}, u32[]{:S(2)}, u32[]{:S(2)}) collective-permute-start(bf16[128,256]{0,1:T(8,128)(2,1)S(1)} %pad_maximum_fusion.1), channel_id=1, source_target_pairs={{0,24},{4,28},{8,32},{12,36},{16,40},{20,44},{24,48},{28,52},{32,5... | collective-permute-start | bytes 196616 | tf_op jit(solution)/shard_map/ppermute | solution.py:14
  93.2 4.3 %collective-permute-start.11 = (bf16[128,256]{0,1:T(8,128)(2,1)S(1)}, bf16[128,256]{0,1:T(8,128)(2,1)S(1)}, u32[]{:S(2)}, u32[]{:S(2)}) collective-permute-start(bf16[128,256]{0,1:T(8,128)(2,1)S(1)} %pad_maximum_fusion.1), channel_id=1, source_target_pairs={{0,20},{4,24},{8,28},{12,32},{16,36},{20,40},{24,44},{28,48},{32,5... | collective-permute-start | bytes 196616 | tf_op jit(solution)/shard_map/ppermute | solution.py:14
  97.5 5.2 %collective-permute-start.12 = (bf16[128,256]{0,1:T(8,128)(2,1)S(1)}, bf16[128,256]{0,1:T(8,128)(2,1)S(1)}, u32[]{:S(2)}, u32[]{:S(2)}) collective-permute-start(bf16[128,256]{0,1:T(8,128)(2,1)S(1)} %pad_maximum_fusion.1), channel_id=1, source_target_pairs={{0,16},{4,20},{8,24},{12,28},{16,32},{20,36},{24,40},{28,44},{32,4... | collective-permute-start | bytes 196616 | tf_op jit(solution)/shard_map/ppermute | solution.py:14
  102.7 3.9 %gather_fusion = bf16[1024,256]{1,0:T(8,128)(2,1)S(1)} fusion(bf16[128,256]{1,0:T(8,128)(2,1)S(1)} %copy.46, s32[1024]{0:T(1024)S(1)} %get-tuple-element.27), kind=kCustom, calls=%fused_computation.clone | custom fusion | bytes 1052672 | tf_op jit(solution)/shard_map/jit(_take)/gather | solution.py:136
  107.3 3.9 %gather_fusion.1 = bf16[1024,256]{1,0:T(8,128)(2,1)S(1)} fusion(bf16[128,256]{1,0:T(8,128)(2,1)S(1)} %copy.46, s32[1024]{0:T(1024)S(1)} %get-tuple-element.28), kind=kCustom, calls=%fused_computation.1.clone | custom fusion | bytes 1052672 | tf_op jit(solution)/shard_map/jit(_take)/gather | solution.py:136
  111.9 3.2 %pad_maximum_fusion = bf16[2,128,2048]{2,0,1:T(2,128)(2,1)} fusion(bf16[1,128,2048]{2,0,1:T(2,128)(2,1)S(1)} %stack_reshape.9, bf16[1,128,2048]{2,0,1:T(2,128)(2,1)S(1)} %stack_reshape.8), kind=kLoop, calls=%fused_computation.17 | loop fusion | flops 2097152 | bytes 2097152 | tf_op jit(solution)/shard_map/stack | solution.py:139
  115.1 8.1 %all-to-all-start.1 = ((bf16[2,128,2048]{2,0,1:T(2,128)(2,1)}), bf16[2,128,2048]{2,0,1:T(2,128)(2,1)S(1)}, u32[]{:S(2)}, u32[]{:S(2)}) async-start(bf16[2,128,2048]{2,0,1:T(2,128)(2,1)} %pad_maximum_fusion), calls=%async_computation.1 | async-start | bytes 2097152 | tf_op jit(solution)/shard_map/all_to_all | solution.py:139
  123.3 3.1 %collective-permute-start.13 = (bf16[128,256]{0,1:T(8,128)(2,1)S(1)}, bf16[128,256]{0,1:T(8,128)(2,1)S(1)}, u32[]{:S(2)}, u32[]{:S(2)}) collective-permute-start(bf16[128,256]{0,1:T(8,128)(2,1)S(1)} %pad_maximum_fusion.1), channel_id=1, source_target_pairs={{0,12},{4,16},{8,20},{12,24},{16,28},{20,32},{24,36},{28,40},{32,4... | collective-permute-start | bytes 196616 | tf_op jit(solution)/shard_map/ppermute | solution.py:14
  127.2 4.6 %collective-permute-start.14 = (bf16[128,256]{0,1:T(8,128)(2,1)S(1)}, bf16[128,256]{0,1:T(8,128)(2,1)S(1)}, u32[]{:S(2)}, u32[]{:S(2)}) collective-permute-start(bf16[128,256]{0,1:T(8,128)(2,1)S(1)} %pad_maximum_fusion.1), channel_id=1, source_target_pairs={{0,8},{4,12},{8,16},{12,20},{16,24},{20,28},{24,32},{28,36},{32,40... | collective-permute-start | bytes 196616 | tf_op jit(solution)/shard_map/ppermute | solution.py:14
  134.2 13.7 %collective-permute-done.13 = bf16[128,256]{0,1:T(8,128)(2,1)S(1)} collective-permute-done((bf16[128,256]{0,1:T(8,128)(2,1)S(1)}, bf16[128,256]{0,1:T(8,128)(2,1)S(1)}, u32[]{:S(2)}, u32[]{:S(2)}) %collective-permute-start.13) | collective-permute-done | bytes 65568 | tf_op jit(solution)/shard_map/ppermute | solution.py:14
  147.9 2.5 %collective-permute-done.14 = bf16[128,256]{0,1:T(8,128)(2,1)S(1)} collective-permute-done((bf16[128,256]{0,1:T(8,128)(2,1)S(1)}, bf16[128,256]{0,1:T(8,128)(2,1)S(1)}, u32[]{:S(2)}, u32[]{:S(2)}) %collective-permute-start.14) | collective-permute-done | bytes 65568 | tf_op jit(solution)/shard_map/ppermute | solution.py:14
  157.9 49.3 %all-gather.7.cloned.1.call-done = bf16[128,12,384]{2,1,0:T(8,128)(2,1)} async-done(((bf16[1,12,384]{2,1,0:T(8,128)(2,1)}), bf16[128,12,384]{2,1,0:T(8,128)(2,1)}) %all-gather.7.cloned.1.call-update) | async-done | bytes 1179664 | tf_op jit(solution)/shard_map/all_gather | solution.py:113
  214.3 23.6 %reduce-scatter.4.cloned.1.call-done = bf16[384,128]{1,0:T(8,128)(2,1)} async-done(((bf16[1536,128]{1,0:T(8,128)(2,1)}), bf16[384,128]{1,0:T(8,128)(2,1)}) %reduce-scatter.4.cloned.1.call-update) | async-done | bytes 98320
  (118 shorter events, 38.0 us)
Async XLA Ops:
  7.2 143.9 %all-gather.5.cloned.1.call-start = ((), (), s32[]{:S(2)}) async-start(), calls=%async_computation.3 | async-start | bytes 1585152 | tf_op jit(solution)/shard_map/all_gather | solution.py:60
  7.9 51.7 %collective-permute-start = (s32[128]{0:T(128)}, s32[128]{0:T(128)S(1)}, u32[]{:S(2)}, u32[]{:S(2)}) collective-permute-start(s32[128]{0:T(128)} %param.15), channel_id=1, source_target_pairs={{0,32},{4,36},{8,40},{12,44},{16,48},{20,52},{24,56},{28,60},{32,6... | collective-permute-start | bytes 1544 | tf_op jit(solution)/shard_map/ppermute | solution.py:14
  13.8 48.9 %collective-permute-start.1 = (s32[128]{0:T(128)}, s32[128]{0:T(128)S(1)}, u32[]{:S(2)}, u32[]{:S(2)}) collective-permute-start(s32[128]{0:T(128)} %param.15), channel_id=1, source_target_pairs={{0,28},{4,32},{8,36},{12,40},{16,44},{20,48},{24,52},{28,56},{32,6... | collective-permute-start | bytes 1544 | tf_op jit(solution)/shard_map/ppermute | solution.py:14
  17.6 49.7 %collective-permute-start.2 = (s32[128]{0:T(128)}, s32[128]{0:T(128)S(1)}, u32[]{:S(2)}, u32[]{:S(2)}) collective-permute-start(s32[128]{0:T(128)} %param.15), channel_id=1, source_target_pairs={{0,24},{4,28},{8,32},{12,36},{16,40},{20,44},{24,48},{28,52},{32,5... | collective-permute-start | bytes 1544 | tf_op jit(solution)/shard_map/ppermute | solution.py:14
  24.3 45.0 %collective-permute-start.3 = (s32[128]{0:T(128)}, s32[128]{0:T(128)S(1)}, u32[]{:S(2)}, u32[]{:S(2)}) collective-permute-start(s32[128]{0:T(128)} %param.15), channel_id=1, source_target_pairs={{0,20},{4,24},{8,28},{12,32},{16,36},{20,40},{24,44},{28,48},{32,5... | collective-permute-start | bytes 1544 | tf_op jit(solution)/shard_map/ppermute | solution.py:14
  27.5 42.0 %collective-permute-start.4 = (s32[128]{0:T(128)}, s32[128]{0:T(128)S(1)}, u32[]{:S(2)}, u32[]{:S(2)}) collective-permute-start(s32[128]{0:T(128)} %param.15), channel_id=1, source_target_pairs={{0,16},{4,20},{8,24},{12,28},{16,32},{20,36},{24,40},{28,44},{32,4... | collective-permute-start | bytes 1544 | tf_op jit(solution)/shard_map/ppermute | solution.py:14
  33.7 24.0 %copy-start.9 = (s32[128]{0:T(128)S(1)}, s32[128]{0:T(128)}, u32[]{:S(2)}) copy-start(s32[128]{0:T(128)} %param.15) | copy-start | bytes 1540
  33.7 24.1 %copy-start = (bf16[128,1536]{1,0:T(8,128)(2,1)S(1)}, bf16[128,1536]{1,0:T(8,128)(2,1)}, u32[]{:S(2)}) copy-start(bf16[128,1536]{1,0:T(8,128)(2,1)} %param.10) | copy-start | bytes 1179652
  33.7 25.9 %copy-start.6 = (bf16[1536]{0:T(1024)(128)(2,1)S(1)}, bf16[1536]{0:T(1024)(128)(2,1)}, u32[]{:S(2)}) copy-start(bf16[1536]{0:T(1024)(128)(2,1)} %param.11) | copy-start | bytes 9220
  33.7 46.5 %all-to-all-start = ((bf16[128,12,256]{2,1,0:T(8,128)(2,1)}), bf16[128,12,256]{2,1,0:T(8,128)(2,1)S(1)}, u32[]{:S(2)}, u32[]{:S(2)}) async-start(bf16[128,12,256]{2,1,0:T(8,128)(2,1)} %stack.8), calls=%async_computation | async-start | bytes 2097152 | tf_op jit(solution)/shard_map/all_to_all | solution.py:64
  49.4 157.8 %all-gather.7.cloned.1.call-start = ((), (), s32[]{:S(2)}) async-start(), calls=%async_computation.4 | async-start | bytes 1585152 | tf_op jit(solution)/shard_map/all_gather | solution.py:113
  59.6 12.2 %collective-permute-start.5 = (s32[128]{0:T(128)S(1)}, s32[128]{0:T(128)S(1)}, u32[]{:S(2)}, u32[]{:S(2)}) collective-permute-start(s32[128]{0:T(128)S(1)} %copy-done.9), channel_id=1, source_target_pairs={{0,12},{4,16},{8,20},{12,24},{16,28},{20,32},{24,36},{28,40},{32,4... | collective-permute-start | bytes 1544 | tf_op jit(solution)/shard_map/ppermute | solution.py:14
  62.7 9.6 %collective-permute-start.6 = (s32[128]{0:T(128)S(1)}, s32[128]{0:T(128)S(1)}, u32[]{:S(2)}, u32[]{:S(2)}) collective-permute-start(s32[128]{0:T(128)S(1)} %copy-done.9), channel_id=1, source_target_pairs={{0,8},{4,12},{8,16},{12,20},{16,24},{20,28},{24,32},{28,36},{32,40... | collective-permute-start | bytes 1544 | tf_op jit(solution)/shard_map/ppermute | solution.py:14
  67.3 5.0 %collective-permute-start.7 = (s32[128]{0:T(128)S(1)}, s32[128]{0:T(128)S(1)}, u32[]{:S(2)}, u32[]{:S(2)}) collective-permute-start(s32[128]{0:T(128)S(1)} %copy-done.9), channel_id=1, source_target_pairs={{0,4},{4,8},{8,12},{12,16},{16,20},{20,24},{24,28},{28,32},{32,36}... | collective-permute-start | bytes 1544 | tf_op jit(solution)/shard_map/ppermute | solution.py:14
  81.3 42.0 %collective-permute-start.8 = (bf16[128,256]{0,1:T(8,128)(2,1)S(1)}, bf16[128,256]{0,1:T(8,128)(2,1)}, u32[]{:S(2)}, u32[]{:S(2)}) collective-permute-start(bf16[128,256]{0,1:T(8,128)(2,1)S(1)} %pad_maximum_fusion.1), channel_id=1, source_target_pairs={{0,32},{4,36},{8,40},{12,44},{16,48},{20,52},{24,56},{28,60},{32,6... | collective-permute-start | bytes 196616 | tf_op jit(solution)/shard_map/ppermute | solution.py:14
  85.5 41.8 %collective-permute-start.9 = (bf16[128,256]{0,1:T(8,128)(2,1)S(1)}, bf16[128,256]{0,1:T(8,128)(2,1)S(1)}, u32[]{:S(2)}, u32[]{:S(2)}) collective-permute-start(bf16[128,256]{0,1:T(8,128)(2,1)S(1)} %pad_maximum_fusion.1), channel_id=1, source_target_pairs={{0,28},{4,32},{8,36},{12,40},{16,44},{20,48},{24,52},{28,56},{32,6... | collective-permute-start | bytes 196616 | tf_op jit(solution)/shard_map/ppermute | solution.py:14
  89.5 42.3 %collective-permute-start.10 = (bf16[128,256]{0,1:T(8,128)(2,1)S(1)}, bf16[128,256]{0,1:T(8,128)(2,1)S(1)}, u32[]{:S(2)}, u32[]{:S(2)}) collective-permute-start(bf16[128,256]{0,1:T(8,128)(2,1)S(1)} %pad_maximum_fusion.1), channel_id=1, source_target_pairs={{0,24},{4,28},{8,32},{12,36},{16,40},{20,44},{24,48},{28,52},{32,5... | collective-permute-start | bytes 196616 | tf_op jit(solution)/shard_map/ppermute | solution.py:14
  93.2 40.9 %collective-permute-start.11 = (bf16[128,256]{0,1:T(8,128)(2,1)S(1)}, bf16[128,256]{0,1:T(8,128)(2,1)S(1)}, u32[]{:S(2)}, u32[]{:S(2)}) collective-permute-start(bf16[128,256]{0,1:T(8,128)(2,1)S(1)} %pad_maximum_fusion.1), channel_id=1, source_target_pairs={{0,20},{4,24},{8,28},{12,32},{16,36},{20,40},{24,44},{28,48},{32,5... | collective-permute-start | bytes 196616 | tf_op jit(solution)/shard_map/ppermute | solution.py:14
  97.5 36.6 %collective-permute-start.12 = (bf16[128,256]{0,1:T(8,128)(2,1)S(1)}, bf16[128,256]{0,1:T(8,128)(2,1)S(1)}, u32[]{:S(2)}, u32[]{:S(2)}) collective-permute-start(bf16[128,256]{0,1:T(8,128)(2,1)S(1)} %pad_maximum_fusion.1), channel_id=1, source_target_pairs={{0,16},{4,20},{8,24},{12,28},{16,32},{20,36},{24,40},{28,44},{32,4... | collective-permute-start | bytes 196616 | tf_op jit(solution)/shard_map/ppermute | solution.py:14
  115.1 124.5 %all-to-all-start.1 = ((bf16[2,128,2048]{2,0,1:T(2,128)(2,1)}), bf16[2,128,2048]{2,0,1:T(2,128)(2,1)S(1)}, u32[]{:S(2)}, u32[]{:S(2)}) async-start(bf16[2,128,2048]{2,0,1:T(2,128)(2,1)} %pad_maximum_fusion), calls=%async_computation.1 | async-start | bytes 2097152 | tf_op jit(solution)/shard_map/all_to_all | solution.py:139
  123.2 114.7 %reduce-scatter.4.cloned.1.call-start = ((), (), s32[]{:S(2)}) async-start(), calls=%async_computation.5 | async-start | bytes 491520
  123.3 24.6 %collective-permute-start.13 = (bf16[128,256]{0,1:T(8,128)(2,1)S(1)}, bf16[128,256]{0,1:T(8,128)(2,1)S(1)}, u32[]{:S(2)}, u32[]{:S(2)}) collective-permute-start(bf16[128,256]{0,1:T(8,128)(2,1)S(1)} %pad_maximum_fusion.1), channel_id=1, source_target_pairs={{0,12},{4,16},{8,20},{12,24},{16,28},{20,32},{24,36},{28,40},{32,4... | collective-permute-start | bytes 196616 | tf_op jit(solution)/shard_map/ppermute | solution.py:14
  127.2 23.2 %collective-permute-start.14 = (bf16[128,256]{0,1:T(8,128)(2,1)S(1)}, bf16[128,256]{0,1:T(8,128)(2,1)S(1)}, u32[]{:S(2)}, u32[]{:S(2)}) collective-permute-start(bf16[128,256]{0,1:T(8,128)(2,1)S(1)} %pad_maximum_fusion.1), channel_id=1, source_target_pairs={{0,8},{4,12},{8,16},{12,20},{16,24},{20,28},{24,32},{28,36},{32,40... | collective-permute-start | bytes 196616 | tf_op jit(solution)/shard_map/ppermute | solution.py:14
  131.9 19.1 %collective-permute-start.15 = (bf16[128,256]{0,1:T(8,128)(2,1)S(1)}, bf16[128,256]{0,1:T(8,128)(2,1)S(1)}, u32[]{:S(2)}, u32[]{:S(2)}) collective-permute-start(bf16[128,256]{0,1:T(8,128)(2,1)S(1)} %pad_maximum_fusion.1), channel_id=1, source_target_pairs={{0,4},{4,8},{8,12},{12,16},{16,20},{20,24},{24,28},{28,32},{32,36}... | collective-permute-start | bytes 196616 | tf_op jit(solution)/shard_map/ppermute | solution.py:14
  (7 other events, 30.3 us)
Sparse Core Ops, SparseCore 0:
  11.2 104.8 all-gather.4
  119.3 87.8 all-gather.6
  214.3 23.5 reduce-scatter.3
